TPU v7x, 32 devices: a whole 2x2x4 slice. The times are simulated.
32 devices in a mesh: cells: 8 (over y, x, core), obs: 4 (over z).
Axes of the slice: x: 2, y: 2, z: 4, core: 2. Of those that a mesh axis runs over, the one named last changes fastest.
Arguments:
- histories: bfloat16 [64, 384], P('obs'), may hold values from -6 to 6
- amplitude: bfloat16 [64, 5, 8192], P('obs', None, 'cells'), may hold values from -0.75 to 0.75
- weights: bfloat16 [8192, 256], P('cells'), may hold values from -0.375 to 0.375
- retarded: int32 [64, 64], P('obs', 'cells'), may hold values from 0 to 128
- owner_block: int32 [8192], P('cells'), may hold values from 0 to 7, as said below
- owner_cell: int32 [8192], P('cells'), may hold values from 0 to 16383
- adjoint: float32 [5, 16, 64, 128], P(None, 'cells', 'obs'), may hold values from -6 to 6
- step_size: float32 [16, 64, 128], P('cells', 'obs'), may hold values from 0.1 to 0.6
- jacobian: float32 [8, 3, 5, 5], P('cells'), may hold values from -6 to 6
Outputs:
- adjoint_next: float32 [5, 16, 64, 128], P(None, 'cells', 'obs')
- panel_source: float32 [5, 8192], P(None, 'cells')
Inputs may be any that keep to these rules, and one draw needn't show every extreme that they name: `owner_block`: among each device's 1024 panels at most 512 name one owner block; one owner block, drawn from the seed, is named by exactly 512 panels of every device.
All inputs are finite; a program needn't handle non-finite values.
Results may differ from a plain program's by a relative error of at most 0.0003.
Values sent between devices are 32-bit elements; how exact they have to be, the bound alone decides.
A program may use at most 192 MiB of HBM per device.

v0:
```python
import jax
import jax.numpy as jnp
from jax import lax
from jax.sharding import PartitionSpec as P

SAMPLES = 256
SPAN = 128
COMP = 5
TILE = 128
smoothing = 0.25


def extended(cells, sides, width, closed):
    for axis, dim in sides:
        count = lax.axis_size(axis)
        ends = count if closed else count - 1
        head = lax.slice_in_dim(cells, 0, width, axis=dim)
        tail = lax.slice_in_dim(cells, cells.shape[dim] - width, cells.shape[dim], axis=dim)
        cells = jnp.concatenate(
            [
                lax.ppermute(tail, axis, [(i, (i + 1) % count) for i in range(ends)]),
                cells,
                lax.ppermute(head, axis, [((i + 1) % count, i) for i in range(ends)]),
            ],
            axis=dim,
        )
    return cells


def on_device(
    histories, amplitude, weights, retarded, owner_block, owner_cell, adjoint, step_size, jacobian
):
    tile_count = weights.shape[0] // TILE
    weights_tiled = weights.reshape(tile_count, TILE, SAMPLES)
    observers_local = histories.shape[0]
    history_len = histories.shape[1]
    shifted = jnp.broadcast_to(histories[:, None, :], (observers_local, tile_count, history_len))
    for bit_number in range(SPAN.bit_length()):
        amount = 1 << bit_number
        moved = jnp.concatenate(
            [
                shifted[..., amount:],
                jnp.zeros((observers_local, tile_count, amount), shifted.dtype),
            ],
            axis=2,
        )
        chosen = retarded >> bit_number & 1 == 1
        shifted = jnp.where(chosen[:, :, None], moved, shifted)
    window = shifted[..., :SAMPLES]
    projected = jnp.einsum(
        "tps,ots->otp", weights_tiled, window, preferred_element_type=jnp.float32
    )
    projected = projected.reshape(projected.shape[0], -1)
    partial_value = jnp.sum(amplitude.astype(jnp.float32) * projected[:, None, :], axis=0)
    panel_source = lax.psum(partial_value, "obs")
    my_block = lax.axis_index("cells")
    my_group = lax.axis_index("obs")
    azimuth_local = adjoint.shape[1]
    radial_local = adjoint.shape[2]
    axial_len = adjoint.shape[3]
    radial_all = radial_local * lax.axis_size("obs")
    block_cells = azimuth_local * radial_all * axial_len
    device_cells = azimuth_local * radial_local * axial_len
    target = (owner_block * block_cells + owner_cell).reshape(1, -1)
    empty_field = jnp.zeros((COMP, device_cells), jnp.float32)
    devices = lax.axis_size("cells")
    capacity = 4 * owner_block.shape[0] // devices
    one_hot = (owner_block[:, None] == jnp.arange(devices, dtype=jnp.int32)[None, :]).astype(
        jnp.int32
    )
    slot_rank = jnp.sum(jnp.cumsum(one_hot, axis=0) * one_hot, axis=1) - 1
    slot_of = owner_block * capacity + slot_rank
    outgoing = jnp.zeros((COMP, devices * capacity), jnp.float32).at[:, slot_of].set(panel_source)
    out_index = jnp.full((1, devices * capacity), -1, jnp.int32).at[0, slot_of].set(target[0])
    received, arrivals = (
        lax.all_to_all(outgoing, "cells", split_axis=1, concat_axis=1, tiled=True),
        lax.all_to_all(out_index, "cells", split_axis=1, concat_axis=1, tiled=True),
    )
    flat_index = arrivals[0]
    block_of = flat_index // block_cells
    within = flat_index % block_cells
    azimuth = within // (radial_all * axial_len)
    radius = within // axial_len % radial_all
    axial = within % axial_len
    is_mine = (block_of == my_block) & (radius // radial_local == my_group) & (flat_index >= 0)
    position = (azimuth * radial_local + radius - my_group * radial_local) * axial_len + axial
    landing = jnp.where(is_mine, position, device_cells)
    surface = empty_field.at[:, landing].add(received, mode="drop")
    widened = extended(adjoint, (("cells", 1),), 1, True)
    heightened = extended(adjoint, (("obs", 2),), 1, False)
    deepened = jnp.pad(adjoint, ((0, 0), (0, 0), (0, 0), (1, 1)))
    matrices = jacobian[0]
    neighbours = (
        (widened[:, 2:], widened[:, :-2]),
        (heightened[:, :, 2:], heightened[:, :, :-2]),
        (deepened[..., 2:], deepened[..., :-2]),
    )
    summed = jnp.zeros_like(adjoint)
    for direction in range(3):
        forward, backward = neighbours[direction]
        rotated = jnp.einsum(
            "kc,karz->carz",
            matrices[direction],
            forward - backward,
            precision=lax.Precision.HIGHEST,
        )
        summed = summed + (0.5 * rotated + smoothing * (forward - 2.0 * adjoint + backward))
    adjoint_next = adjoint + step_size[None] * summed + surface.reshape(adjoint.shape)
    return (adjoint_next, panel_source)


def solution(mesh):
    return jax.shard_map(
        on_device,
        mesh=mesh,
        in_specs=(
            P("obs", None),
            P("obs", None, "cells"),
            P("cells", None),
            P("obs", "cells"),
            P("cells"),
            P("cells"),
            P(None, "cells", "obs", None),
            P("cells", "obs", None),
            P("cells", None, None, None),
        ),
        out_specs=(P(None, "cells", "obs", None), P(None, "cells")),
        check_vma=False,
    )
```

profile of v0, /device:TPU:0, one launch (start us, length us, event | category | flops | bytes accessed | tf_op | source)
XLA Modules:
  0.0 93.0 jit_solution(10608358137834040790)
XLA Ops:
  0.6 0.8 fusion.22
  1.4 2.3 %reduce-window.6 = s32[8,8,128]{2,1,0:T(8,128)S(1)} reduce-window(s32[8,8,128]{2,1,0:T(8,128)S(1)} %fusion.22, s32[]{:T(128)} %constant.118.clone.1), window={size=1x1x128 pad=0_0x0_0x127_0}, to_apply=%region_0.1 | reduce-window | flops 1040384 | bytes 65540 | tf_op jit(solution)/shard_map/reduce-window
  3.6 0.3 slice_reduce_fusion
  3.9 0.2 reduce-window.9
  4.1 0.1 add_bitcast_fusion
  4.2 0.7 fusion.21
  4.9 0.7 multiply_add_fusion
  5.6 0.7 fusion.25
  6.3 0.7 and_reduce_fusion
  7.1 4.9 %scatter_custom_fusion.2 = s32[4096]{0:T(1024)} fusion(s32[1024]{0:T(1024)S(1)} %broadcast_select_fusion, s32[1024]{0:T(1024)S(1)} %get-tuple-element.25, s32[]{:T(128)} %constant.116.clone.1), kind=kCustom, calls=%fused_computation.79 | custom fusion | bytes 16388
  12.0 5.2 %all-to-all-start = ((s32[1,8,512]{2,0,1:T(1,128)}), s32[1,8,512]{2,0,1:T(1,128)S(1)}, u32[]{:S(2)}, u32[]{:S(2)}) async-start(s32[1,8,512]{2,0,1:T(1,128)} %bitcast.12), calls=%async_computation | async-start | bytes 32768 | tf_op jit(solution)/shard_map/all_to_all | solution.py:77
  17.2 0.9 %copy.91 = f32[5,2,16,128]{3,0,2,1:T(8,128)S(1)} copy(f32[5,2,16,128]{3,2,1,0:T(8,128)} %param.15) | data formatting | bytes 163840 | tf_op args[6]
  18.1 1.3 %collective-permute-start.2 = (f32[5,2,1,128]{3,0,2,1:T(8,128)S(1)}, f32[5,2,1,128]{3,0,2,1:T(8,128)}, u32[]{:S(2)}, u32[]{:S(2)}) collective-permute-start(f32[5,2,1,128]{3,0,2,1:T(8,128)S(1)} %get-tuple-element.13), channel_id=1, source_target_pairs={{1,0},{2,1},{3,2},{5,4},{6,5},{7,6},{9,8},{10,9},{11,10},{13,12},{... | collective-permute-start | bytes 15368 | tf_op jit(solution)/shard_map/ppermute | solution.py:23
  19.4 5.1 %collective-permute-start.3 = (f32[5,2,1,128]{3,0,2,1:T(8,128)S(1)}, f32[5,2,1,128]{3,0,2,1:T(8,128)}, u32[]{:S(2)}, u32[]{:S(2)}) collective-permute-start(f32[5,2,1,128]{3,0,2,1:T(8,128)S(1)} %get-tuple-element.12), channel_id=1, source_target_pairs={{0,1},{1,2},{2,3},{4,5},{5,6},{6,7},{8,9},{9,10},{10,11},{12,13},{... | collective-permute-start | bytes 15368 | tf_op jit(solution)/shard_map/ppermute | solution.py:21
  24.6 0.6 fusion.32
  25.2 2.1 %collective-permute-start = (f32[5,1,16,128]{3,0,2,1:T(8,128)}, f32[5,1,16,128]{3,0,2,1:T(8,128)S(1)}, u32[]{:S(2)}, u32[]{:S(2)}) collective-permute-start(f32[5,1,16,128]{3,0,2,1:T(8,128)} %get-tuple-element.11), channel_id=1, source_target_pairs={{4,0},{8,4},{12,8},{16,12},{20,16},{24,20},{28,24},{0,28},{5,1},{9... | collective-permute-start | bytes 122888 | tf_op jit(solution)/shard_map/ppermute | solution.py:23
  27.3 0.7 and_compare_fusion.7
  28.0 0.8 slice.95
  28.8 0.8 pad_select_fusion.6
  29.6 0.1 slice.109
  29.7 0.9 pad_select_fusion.5
  30.6 0.1 slice.110
  30.7 0.8 pad_select_fusion.4
  31.5 0.1 slice.111
  31.6 0.1 pad_select_fusion.3
  31.7 0.1 slice.112
  31.8 0.1 pad_select_fusion.2
  31.9 0.1 slice.113
  32.0 0.1 pad_select_fusion.1
  32.1 0.1 slice.114
  32.2 0.1 pad_select_fusion
  32.4 0.3 convolution_bitcast_fusion
  32.6 0.0 copy-done.5
  32.7 1.1 %fusion.10 = f32[5,2,16,128]{3,0,2,1:T(8,128)} fusion(f32[5,2,16,128]{3,0,2,1:T(8,128)S(1)} %copy.91, f32[1,1,5,5]{3,0,2,1:T(1,128)S(1)} %get-tuple-element.16), kind=kOutput, calls=%fused_computation.16 | convolution fusion | flops 1372160 | bytes 346624 | tf_op jit(solution)/shard_map/kc,karz->carz/dot_general | solution.py:101
  33.8 0.1 multiply_reduce_fusion
  33.8 17.3 %psum.7 = f32[5,1024]{1,0:T(8,128)S(1)} all-reduce(f32[5,1024]{1,0:T(8,128)S(1)} %multiply_reduce_fusion), channel_id=1, replica_groups=mesh['cells'=8,'obs'=4] {'obs'}, use_global_device_ids=true, to_apply=%region_5.6 | all-reduce | flops 5120 | bytes 40960 | tf_op jit(solution)/shard_map/psum | solution.py:55
  51.2 0.2 copy.93
  51.4 3.6 %scatter_custom_fusion = f32[5,4096]{0,1:T(8,128)S(1)} fusion(s32[1024]{0:T(1024)S(1)} %get-tuple-element.26, f32[1024,5]{1,0:T(8,128)S(1)} %copy.93, f32[]{:T(128)} %constant.115.clone.1), kind=kCustom, calls=%fused_computation.20 | custom fusion | bytes 81924 | tf_op jit(solution)/shard_map/scatter | solution.py:73
  55.0 1.3 %copy.94 = f32[5,8,512]{2,0,1:T(8,128)} copy(f32[5,8,512]{0,2,1:T(8,128)S(1)} %bitcast.73) | data formatting | bytes 163840 | tf_op jit(solution)/shard_map/all_to_all | solution.py:76
  56.3 1.1 %fusion.9 = f32[5,2,16,128]{3,0,2,1:T(8,128)S(1)} fusion(f32[5,2,1,128]{3,0,2,1:T(8,128)} %collective-permute-done.2, f32[5,2,16,128]{3,0,2,1:T(8,128)S(1)} %copy.91, f32[5,2,1,128]{3,0,2,1:T(8,128)} %collective-permute-done.3, f32[1,1,5,5]{3,0,2,1:T(1,128)S(1)} %get-tuple-element.15), kind=kOutput, calls=%fused_computation.15 | convolution fusion | flops 1454080 | bytes 174180 | tf_op jit(solution)/shard_map/kc,karz->carz/dot_general | solution.py:101
  57.4 3.4 %all-to-all-start.1 = ((f32[5,8,512]{2,0,1:T(8,128)}), f32[5,8,512]{2,0,1:T(8,128)S(1)}, u32[]{:S(2)}, u32[]{:S(2)}) async-start(f32[5,8,512]{2,0,1:T(8,128)} %copy.94), calls=%async_computation.1 | async-start | bytes 262144 | tf_op jit(solution)/shard_map/all_to_all | solution.py:76
  60.8 0.5 compare_select_fusion
  61.3 5.0 %all-to-all-done.1 = f32[5,8,512]{2,0,1:T(8,128)S(1)} async-done(((f32[5,8,512]{2,0,1:T(8,128)}), f32[5,8,512]{2,0,1:T(8,128)S(1)}, u32[]{:S(2)}, u32[]{:S(2)}) %all-to-all-start.1) | async-done | bytes 81952 | tf_op jit(solution)/shard_map/all_to_all | solution.py:76
  66.2 2.0 %copy.95 = f32[4096,5]{1,0:T(8,128)} copy(f32[4096,5]{0,1:T(8,128)S(1)} %bitcast.74) | data formatting | bytes 163840 | tf_op jit(solution)/shard_map/all_to_all | solution.py:76
  68.2 23.2 %scatter_custom_fusion.1 = f32[5,4096]{0,1:T(8,128)S(1)} fusion(s32[4096]{0:T(1024)S(1)} %bitcast.82, f32[4096,5]{1,0:T(8,128)} %copy.95, f32[]{:T(128)} %constant.115.clone.1), kind=kCustom, calls=%fused_computation.18 | custom fusion | flops 20480 | bytes 82432 | tf_op jit(solution)/shard_map/scatter-add | solution.py:88
  91.4 0.6 copy.97
  92.0 0.3 fusion.8
  92.4 0.7 copy.98
  (23 shorter events, 0.1 us)
Async XLA Ops:
  0.6 31.7 %copy-start = (bf16[1024,256]{1,0:T(8,128)(2,1)S(1)}, bf16[1024,256]{1,0:T(8,128)(2,1)}, u32[]{:S(2)}) copy-start(bf16[1024,256]{1,0:T(8,128)(2,1)} %param.11) | copy-start | bytes 1572868
  12.0 45.4 %all-to-all-start = ((s32[1,8,512]{2,0,1:T(1,128)}), s32[1,8,512]{2,0,1:T(1,128)S(1)}, u32[]{:S(2)}, u32[]{:S(2)}) async-start(s32[1,8,512]{2,0,1:T(1,128)} %bitcast.12), calls=%async_computation | async-start | bytes 32768 | tf_op jit(solution)/shard_map/all_to_all | solution.py:77
  18.1 38.1 %collective-permute-start.2 = (f32[5,2,1,128]{3,0,2,1:T(8,128)S(1)}, f32[5,2,1,128]{3,0,2,1:T(8,128)}, u32[]{:S(2)}, u32[]{:S(2)}) collective-permute-start(f32[5,2,1,128]{3,0,2,1:T(8,128)S(1)} %get-tuple-element.13), channel_id=1, source_target_pairs={{1,0},{2,1},{3,2},{5,4},{6,5},{7,6},{9,8},{10,9},{11,10},{13,12},{... | collective-permute-start | bytes 15368 | tf_op jit(solution)/shard_map/ppermute | solution.py:23
  19.4 36.9 %collective-permute-start.3 = (f32[5,2,1,128]{3,0,2,1:T(8,128)S(1)}, f32[5,2,1,128]{3,0,2,1:T(8,128)}, u32[]{:S(2)}, u32[]{:S(2)}) collective-permute-start(f32[5,2,1,128]{3,0,2,1:T(8,128)S(1)} %get-tuple-element.12), channel_id=1, source_target_pairs={{0,1},{1,2},{2,3},{4,5},{5,6},{6,7},{8,9},{9,10},{10,11},{12,13},{... | collective-permute-start | bytes 15368 | tf_op jit(solution)/shard_map/ppermute | solution.py:21
  25.2 66.8 %collective-permute-start = (f32[5,1,16,128]{3,0,2,1:T(8,128)}, f32[5,1,16,128]{3,0,2,1:T(8,128)S(1)}, u32[]{:S(2)}, u32[]{:S(2)}) collective-permute-start(f32[5,1,16,128]{3,0,2,1:T(8,128)} %get-tuple-element.11), channel_id=1, source_target_pairs={{4,0},{8,4},{12,8},{16,12},{20,16},{24,20},{28,24},{0,28},{5,1},{9... | collective-permute-start | bytes 122888 | tf_op jit(solution)/shard_map/ppermute | solution.py:23
  27.3 64.7 %collective-permute-start.1 = (f32[5,1,16,128]{3,0,2,1:T(8,128)S(1)}, f32[5,1,16,128]{3,0,2,1:T(8,128)S(1)}, u32[]{:S(2)}, u32[]{:S(2)}) collective-permute-start(f32[5,1,16,128]{3,0,2,1:T(8,128)S(1)} %get-tuple-element.10), channel_id=1, source_target_pairs={{0,4},{4,8},{8,12},{12,16},{16,20},{20,24},{24,28},{28,0},{1,5},{5... | collective-permute-start | bytes 122888 | tf_op jit(solution)/shard_map/ppermute | solution.py:21
  28.8 3.9 %copy-start.5 = (f32[1,3,5,5]{3,0,2,1:T(1,128)S(1)}, f32[1,3,5,5]{3,0,2,1:T(1,128)}, u32[]{:S(2)}) copy-start(f32[1,3,5,5]{3,0,2,1:T(1,128)} %param.17) | copy-start | bytes 904
  29.7 4.0 %copy-start.1 = (bf16[16,5,1024]{2,0,1:T(8,128)(2,1)S(1)}, bf16[16,5,1024]{2,0,1:T(8,128)(2,1)}, u32[]{:S(2)}) copy-start(bf16[16,5,1024]{2,0,1:T(8,128)(2,1)} %param.10) | copy-start | bytes 491524
  51.2 5.1 %copy-start.2 = (f32[5,1024]{1,0:T(8,128)}, f32[5,1024]{1,0:T(8,128)S(1)}, u32[]{:S(2)}) copy-start(f32[5,1024]{1,0:T(8,128)S(1)} %psum.7) | copy-start | bytes 61444
  57.4 8.8 %all-to-all-start.1 = ((f32[5,8,512]{2,0,1:T(8,128)}), f32[5,8,512]{2,0,1:T(8,128)S(1)}, u32[]{:S(2)}, u32[]{:S(2)}) async-start(f32[5,8,512]{2,0,1:T(8,128)} %copy.94), calls=%async_computation.1 | async-start | bytes 262144 | tf_op jit(solution)/shard_map/all_to_all | solution.py:76
  68.2 23.8 %copy-start.3 = (f32[5,2,16,128]{3,0,2,1:T(8,128)S(1)}, f32[5,2,16,128]{3,0,2,1:T(8,128)}, u32[]{:S(2)}) copy-start(f32[5,2,16,128]{3,0,2,1:T(8,128)} %fusion.10) | copy-start | bytes 245764
  68.2 23.8 %copy-start.4 = (f32[2,16,128]{2,1,0:T(8,128)S(1)}, f32[2,16,128]{2,1,0:T(8,128)}, u32[]{:S(2)}) copy-start(f32[2,16,128]{2,1,0:T(8,128)} %param.16) | copy-start | bytes 49156
where the time goes:
time: 94.1 us; the launch traced here: 93 us
  other arithmetic  33.4 us (35%)
  blocking collectives  17.3 us (18%)
  starting transfers between devices  17.1 us (18%)
  local copies, waits for them, and re-layouts  16.5 us (18%)
  waiting for transfers between devices  4.98 us (5%)
  matrix products  2.79 us (3%)
    scatter-add x1, other arithmetic, on_device(): surface = empty_field.at[:, landing].add(received, mode='drop')  23.2 us
    psum x1, blocking collectives, on_device(): panel_source = lax.psum(partial_value, 'obs')  17.3 us
    unnamed x15, local copies, waits for them, and re-layouts  6.53 us
    all_to_all x1, starting transfers between devices, on_device(): lax.all_to_all(out_index, 'cells', split_axis=1, concat_axis=1, tiled=True)  5.2 us
    ppermute x2, starting transfers between devices, extended(): lax.ppermute(tail, axis, [(i, (i + 1) % count) for i in range(ends)])  5.15 us
    all_to_all x1, waiting for transfers between devices, on_device(): lax.all_to_all(outgoing, 'cells', split_axis=1, concat_axis=1, tiled=True)  4.97 us
    scatter x1, local copies, waits for them, and re-layouts, on_device(): jnp.zeros((COMP, devices * capacity), jnp.float32).at[:, slot_of]  3.59 us
    all_to_all x1, starting transfers between devices, on_device(): lax.all_to_all(outgoing, 'cells', split_axis=1, concat_axis=1, tiled=True)  3.38 us
  transfers between devices with their start and end apart: 6, of which 1 were waited for; matrix products, arithmetic and copies ran while one was open for 43% of the time, Pallas kernels for 0%

commit v1 on v0

--- a/solution.py
+++ b/solution.py
@@ -52,7 +52,11 @@
     )
     projected = projected.reshape(projected.shape[0], -1)
     partial_value = jnp.sum(amplitude.astype(jnp.float32) * projected[:, None, :], axis=0)
-    panel_source = lax.psum(partial_value, "obs")
+    panel_source = partial_value
+    for hop in (1, 2):
+        panel_source = panel_source + lax.ppermute(
+            panel_source, "obs", [(dev, dev ^ hop) for dev in range(4)]
+        )
     my_block = lax.axis_index("cells")
     my_group = lax.axis_index("obs")
     azimuth_local = adjoint.shape[1]

time: 94.1 us -> 77.1 us (0.82)
  blocking collectives: 17.3 us -> 0 us
  starting transfers between devices: 17.1 us -> 20.8 us
  other arithmetic: 33.4 us -> 30 us
  waiting for transfers between devices: 4.98 us -> 6.24 us
    psum x1 -> x0, blocking collectives: 17.3 us -> none  [on_device(): panel_source = lax.psum(partial_value, 'obs')]
    ppermute x0 -> x2, starting transfers between devices: none -> 5.77 us  [on_device(): lax.ppermute(panel_source, 'obs', [(dev, dev ^ hop) for dev in range(4)])]
    all_to_all x1, starting transfers between devices: 5.2 us -> 3.72 us  [on_device(): lax.all_to_all(out_index, 'cells', split_axis=1, concat_axis=1, tiled=True)]
    unnamed x4, other arithmetic: 1.57 us -> 0.26 us
    ppermute x0 -> x2, waiting for transfers between devices: none -> 1.26 us  [on_device(): lax.ppermute(panel_source, 'obs', [(dev, dev ^ hop) for dev in range(4)])]
    unnamed x15 -> x27, local copies, waits for them, and re-layouts: 6.53 us -> 5.68 us
  transfers between devices with their start and end apart: 6 -> 8, of which waited for: 1 -> 2; matrix products, arithmetic and copies ran while one was open for 43% -> 55% of each run, Pallas kernels for 0% -> 0%
where the time goes in v1:
time: 77.1 us; the launch traced here: 76.4 us
  other arithmetic  30 us (39%)
  starting transfers between devices  20.8 us (27%)
  local copies, waits for them, and re-layouts  15.7 us (20%)
  waiting for transfers between devices  6.24 us (8%)
  matrix products  2.66 us (3%)
  between operations  1.01 us (1%)
    scatter-add x1, other arithmetic, on_device(): surface = empty_field.at[:, landing].add(received, mode='drop')  23.2 us
    ppermute x2, starting transfers between devices, on_device(): lax.ppermute(panel_source, 'obs', [(dev, dev ^ hop) for dev in range(4)])  5.77 us
    unnamed x27, local copies, waits for them, and re-layouts  5.68 us
    all_to_all x1, waiting for transfers between devices, on_device(): lax.all_to_all(outgoing, 'cells', split_axis=1, concat_axis=1, tiled=True)  4.97 us
    ppermute x2, starting transfers between devices, extended(): lax.ppermute(tail, axis, [(i, (i + 1) % count) for i in range(ends)])  4.55 us
    all_to_all x1, starting transfers between devices, on_device(): lax.all_to_all(out_index, 'cells', split_axis=1, concat_axis=1, tiled=True)  3.72 us
    scatter x1, local copies, waits for them, and re-layouts, on_device(): jnp.zeros((COMP, devices * capacity), jnp.float32).at[:, slot_of]  3.59 us
    all_to_all x1, starting transfers between devices, on_device(): lax.all_to_all(outgoing, 'cells', split_axis=1, concat_axis=1, tiled=True)  3.37 us
  transfers between devices with their start and end apart: 8, of which 2 were waited for; matrix products, arithmetic and copies ran while one was open for 55% of the time, Pallas kernels for 0%

profile of v1, /device:TPU:0, one launch (start us, length us, event | category | flops | bytes accessed | tf_op | source)
XLA Modules:
  0.0 76.4 jit_solution(1670030182117314516)
XLA Ops:
  0.6 0.0 copy-start
  0.6 0.8 and_compare_fusion.7
  1.4 0.8 %slice.95 = bf16[16,383]{1,0:T(8,128)(2,1)S(1)} slice(bf16[16,384]{1,0:T(8,128)(2,1)} %param.9), slice={[0:16], [1:384]} | slice | bytes 24512 | tf_op jit(solution)/shard_map/slice | solution.py:42
  2.2 0.8 %pad_select_fusion.6 = bf16[16,8,384]{2,0,1:T(8,128)(2,1)S(1)} fusion(bf16[16,8,383]{2,0,1:T(8,128)(2,1)S(1)} %broadcast_in_dim.94, pred[16,8]{0,1:T(8,128)(4,1)S(1)} %get-tuple-element.23, bf16[16,384]{1,0:T(8,128)(2,1)} %param.9), kind=kLoop, calls=%fused_computation.38 | loop fusion | flops 49152 | bytes 208768 | tf_op jit(solution)/shard_map/jit(_where)/select_n | solution.py:48
  3.1 0.1 slice.109
  3.2 0.8 %pad_select_fusion.5 = bf16[16,8,384]{2,0,1:T(8,128)(2,1)S(1)} fusion(bf16[16,8,382]{2,0,1:T(8,128)(2,1)S(1)} %slice.109, pred[16,8]{0,1:T(8,128)(4,1)S(1)} %get-tuple-element.24, bf16[16,384]{1,0:T(8,128)(2,1)} %param.9, bf16[16,8,383]{2,0,1:T(8,128)(2,1)S(1)} %broadcast_in_dim.94, pred[16,8]{0,1:T(8,128)(4,1)S(1)} %get-tuple-element.23), kind=kLoop, calls=%fused_computation.37 | loop fusion | flops 98304 | bytes 306688 | tf_op jit(solution)/shard_map/jit(_where)/select_n | solution.py:48
  4.0 0.1 slice.110
  4.1 0.8 %pad_select_fusion.4 = bf16[16,8,384]{2,0,1:T(8,128)(2,1)S(1)} fusion(bf16[16,8,380]{2,0,1:T(8,128)(2,1)S(1)} %slice.110, pred[16,8]{0,1:T(8,128)(4,1)S(1)} %get-tuple-element.18, bf16[16,384]{1,0:T(8,128)(2,1)} %param.9, bf16[16,8,383]{2,0,1:T(8,128)(2,1)S(1)} %broadcast_in_dim.94, pred[16,8]{0,1:T(8,128)(4,1)S(1)} %get-tuple-element.23, ...), kind=kLoop, calls=%fused_computation.36 | loop fusion | flops 147456 | bytes 404096 | tf_op jit(solution)/shard_map/jit(_where)/select_n | solution.py:48
  5.0 0.1 slice.111
  5.1 0.1 pad_select_fusion.3
  5.2 0.1 slice.112
  5.3 0.1 pad_select_fusion.2
  5.4 0.1 slice.113
  5.5 0.1 pad_select_fusion.1
  5.6 0.1 slice.114
  5.7 0.1 pad_select_fusion
  5.8 0.3 convolution_bitcast_fusion
  6.1 0.0 copy-done.1
  6.1 0.1 multiply_reduce_fusion
  6.2 3.1 %collective-permute-start.4 = (f32[5,1024]{1,0:T(8,128)S(1)}, f32[5,1024]{1,0:T(8,128)S(1)}, u32[]{:S(2)}, u32[]{:S(2)}) collective-permute-start(f32[5,1024]{1,0:T(8,128)S(1)} %multiply_reduce_fusion), channel_id=1, source_target_pairs={{0,1},{1,0},{2,3},{3,2},{4,5},{5,4},{6,7},{7,6},{8,9},{9,8},{10,11... | collective-permute-start | bytes 61448 | tf_op jit(solution)/shard_map/ppermute | solution.py:57
  9.3 2.3 %reduce-window.6 = s32[8,8,128]{2,1,0:T(8,128)S(1)} reduce-window(s32[8,8,128]{2,1,0:T(8,128)S(1)} %fusion.22, s32[]{:T(128)} %constant.118.clone.1), window={size=1x1x128 pad=0_0x0_0x127_0}, to_apply=%region_0.1 | reduce-window | flops 1040384 | bytes 65540 | tf_op jit(solution)/shard_map/reduce-window
  11.6 0.3 slice_reduce_fusion
  11.9 0.2 reduce-window.9
  12.1 0.1 add_bitcast_fusion
  12.2 0.1 fusion.25
  12.3 0.1 and_reduce_fusion
  12.4 4.9 %scatter_custom_fusion.2 = s32[4096]{0:T(1024)} fusion(s32[1024]{0:T(1024)S(1)} %broadcast_select_fusion, s32[1024]{0:T(1024)S(1)} %get-tuple-element.25, s32[]{:T(128)} %constant.116.clone.1), kind=kCustom, calls=%fused_computation.79 | custom fusion | bytes 16388
  17.3 3.7 %all-to-all-start = ((s32[1,8,512]{2,0,1:T(1,128)}), s32[1,8,512]{2,0,1:T(1,128)S(1)}, u32[]{:S(2)}, u32[]{:S(2)}) async-start(s32[1,8,512]{2,0,1:T(1,128)} %bitcast.12), calls=%async_computation | async-start | bytes 32768 | tf_op jit(solution)/shard_map/all_to_all | solution.py:81
  21.0 0.1 copy.91
  21.1 1.3 %collective-permute-start.2 = (f32[5,2,1,128]{3,0,2,1:T(8,128)S(1)}, f32[5,2,1,128]{3,0,2,1:T(8,128)S(1)}, u32[]{:S(2)}, u32[]{:S(2)}) collective-permute-start(f32[5,2,1,128]{3,0,2,1:T(8,128)S(1)} %get-tuple-element.13), channel_id=1, source_target_pairs={{1,0},{2,1},{3,2},{5,4},{6,5},{7,6},{9,8},{10,9},{11,10},{13,12},{... | collective-permute-start | bytes 15368 | tf_op jit(solution)/shard_map/ppermute | solution.py:23
  22.4 4.5 %collective-permute-start.3 = (f32[5,2,1,128]{3,0,2,1:T(8,128)S(1)}, f32[5,2,1,128]{3,0,2,1:T(8,128)S(1)}, u32[]{:S(2)}, u32[]{:S(2)}) collective-permute-start(f32[5,2,1,128]{3,0,2,1:T(8,128)S(1)} %get-tuple-element.12), channel_id=1, source_target_pairs={{0,1},{1,2},{2,3},{4,5},{5,6},{6,7},{8,9},{9,10},{10,11},{12,13},{... | collective-permute-start | bytes 15368 | tf_op jit(solution)/shard_map/ppermute | solution.py:21
  26.9 0.6 fusion.32
  27.6 2.1 %collective-permute-start = (f32[5,1,16,128]{3,0,2,1:T(8,128)}, f32[5,1,16,128]{3,0,2,1:T(8,128)S(1)}, u32[]{:S(2)}, u32[]{:S(2)}) collective-permute-start(f32[5,1,16,128]{3,0,2,1:T(8,128)} %get-tuple-element.11), channel_id=1, source_target_pairs={{4,0},{8,4},{12,8},{16,12},{20,16},{24,20},{28,24},{0,28},{5,1},{9... | collective-permute-start | bytes 122888 | tf_op jit(solution)/shard_map/ppermute | solution.py:23
  29.7 1.1 %fusion.10 = f32[5,2,16,128]{3,0,2,1:T(8,128)} fusion(f32[5,2,16,128]{3,0,2,1:T(8,128)S(1)} %copy.91, f32[1,1,5,5]{3,0,2,1:T(1,128)S(1)} %get-tuple-element.16), kind=kOutput, calls=%fused_computation.16 | convolution fusion | flops 1372160 | bytes 346624 | tf_op jit(solution)/shard_map/kc,karz->carz/dot_general | solution.py:105
  30.7 2.7 %collective-permute-start.5 = (f32[5,1024]{1,0:T(8,128)S(1)}, f32[5,1024]{1,0:T(8,128)S(1)}, u32[]{:S(2)}, u32[]{:S(2)}) collective-permute-start(f32[5,1024]{1,0:T(8,128)S(1)} %add.185), channel_id=1, source_target_pairs={{0,2},{1,3},{2,0},{3,1},{4,6},{5,7},{6,4},{7,5},{8,10},{9,11},{10,... | collective-permute-start | bytes 61448 | tf_op jit(solution)/shard_map/ppermute | solution.py:57
  33.4 1.0 %fusion.9 = f32[5,2,16,128]{3,0,2,1:T(8,128)} fusion(f32[5,2,1,128]{3,0,2,1:T(8,128)S(1)} %collective-permute-done.2, f32[5,2,16,128]{3,0,2,1:T(8,128)S(1)} %copy.91, f32[5,2,1,128]{3,0,2,1:T(8,128)S(1)} %collective-permute-done.3, f32[1,1,5,5]{3,0,2,1:T(1,128)S(1)} %get-tuple-element.15), kind=kOutput, calls=%fused_computation.15 | convolution fusion | flops 1454080 | bytes 174180 | tf_op jit(solution)/shard_map/kc,karz->carz/dot_general | solution.py:105
  34.4 1.3 %collective-permute-done.5 = f32[5,1024]{1,0:T(8,128)S(1)} collective-permute-done((f32[5,1024]{1,0:T(8,128)S(1)}, f32[5,1024]{1,0:T(8,128)S(1)}, u32[]{:S(2)}, u32[]{:S(2)}) %collective-permute-start.5) | collective-permute-done | bytes 20512 | tf_op jit(solution)/shard_map/ppermute | solution.py:57
  35.6 0.2 copy.93
  35.9 3.6 %scatter_custom_fusion = f32[5,4096]{0,1:T(8,128)S(1)} fusion(s32[1024]{0:T(1024)S(1)} %get-tuple-element.26, f32[1024,5]{1,0:T(8,128)S(1)} %copy.93, f32[]{:T(128)} %constant.115.clone.1), kind=kCustom, calls=%fused_computation.20 | custom fusion | bytes 81924 | tf_op jit(solution)/shard_map/scatter | solution.py:77
  39.5 1.3 %copy.94 = f32[5,8,512]{2,0,1:T(8,128)} copy(f32[5,8,512]{0,2,1:T(8,128)S(1)} %bitcast.73) | data formatting | bytes 163840 | tf_op jit(solution)/shard_map/all_to_all | solution.py:80
  40.7 3.4 %all-to-all-start.1 = ((f32[5,8,512]{2,0,1:T(8,128)}), f32[5,8,512]{2,0,1:T(8,128)S(1)}, u32[]{:S(2)}, u32[]{:S(2)}) async-start(f32[5,8,512]{2,0,1:T(8,128)} %copy.94), calls=%async_computation.1 | async-start | bytes 262144 | tf_op jit(solution)/shard_map/all_to_all | solution.py:80
  44.1 0.5 compare_select_fusion
  44.6 5.0 %all-to-all-done.1 = f32[5,8,512]{2,0,1:T(8,128)S(1)} async-done(((f32[5,8,512]{2,0,1:T(8,128)}), f32[5,8,512]{2,0,1:T(8,128)S(1)}, u32[]{:S(2)}, u32[]{:S(2)}) %all-to-all-start.1) | async-done | bytes 81952 | tf_op jit(solution)/shard_map/all_to_all | solution.py:80
  49.6 2.0 %copy.95 = f32[4096,5]{1,0:T(8,128)} copy(f32[4096,5]{0,1:T(8,128)S(1)} %bitcast.74) | data formatting | bytes 163840 | tf_op jit(solution)/shard_map/all_to_all | solution.py:80
  51.6 23.2 %scatter_custom_fusion.1 = f32[5,4096]{0,1:T(8,128)S(1)} fusion(s32[4096]{0:T(1024)S(1)} %bitcast.82, f32[4096,5]{1,0:T(8,128)} %copy.95, f32[]{:T(128)} %constant.115.clone.1), kind=kCustom, calls=%fused_computation.18 | custom fusion | flops 20480 | bytes 82432 | tf_op jit(solution)/shard_map/scatter-add | solution.py:92
  74.7 0.6 copy.97
  75.4 0.3 fusion.8
  75.7 0.7 copy.98
  (40 shorter events, 0.2 us)
Async XLA Ops:
  0.6 5.2 %copy-start = (bf16[1024,256]{1,0:T(8,128)(2,1)S(1)}, bf16[1024,256]{1,0:T(8,128)(2,1)}, u32[]{:S(2)}) copy-start(bf16[1024,256]{1,0:T(8,128)(2,1)} %param.11) | copy-start | bytes 1572868
  2.2 3.9 %copy-start.1 = (bf16[16,5,1024]{2,0,1:T(8,128)(2,1)S(1)}, bf16[16,5,1024]{2,0,1:T(8,128)(2,1)}, u32[]{:S(2)}) copy-start(bf16[16,5,1024]{2,0,1:T(8,128)(2,1)} %param.10) | copy-start | bytes 491524
  3.2 6.2 %copy-start.6 = (s32[1024]{0:T(1024)S(1)}, s32[1024]{0:T(1024)}, u32[]{:S(2)}) copy-start(s32[1024]{0:T(1024)} %param.13) | copy-start | bytes 12292
  4.0 8.2 %copy-start.9 = (s32[1024]{0:T(1024)S(1)}, s32[1024]{0:T(1024)}, u32[]{:S(2)}) copy-start(s32[1024]{0:T(1024)} %param.14) | copy-start | bytes 12292
  4.0 8.2 %copy-start.10 = (s32[2]{0:T(128)S(1)}, s32[2]{0:T(128)}, u32[]{:S(2)}) copy-start(s32[2]{0:T(128)} %constant.165) | copy-start | bytes 28
  4.0 8.3 %copy-start.11 = (s32[2]{0:T(128)S(1)}, s32[2]{0:T(128)}, u32[]{:S(2)}) copy-start(s32[2]{0:T(128)} %constant.168) | copy-start | bytes 28
  4.0 17.0 %copy-start.5 = (f32[5,2,16,128]{3,2,1,0:T(8,128)S(1)}, f32[5,2,16,128]{3,2,1,0:T(8,128)}, u32[]{:S(2)}) copy-start(f32[5,2,16,128]{3,2,1,0:T(8,128)} %param.15) | copy-start | bytes 245764
  5.0 24.7 %copy-start.8 = (f32[1,3,5,5]{3,0,2,1:T(1,128)S(1)}, f32[1,3,5,5]{3,0,2,1:T(1,128)}, u32[]{:S(2)}) copy-start(f32[1,3,5,5]{3,0,2,1:T(1,128)} %param.17) | copy-start | bytes 904
  6.2 24.5 %collective-permute-start.4 = (f32[5,1024]{1,0:T(8,128)S(1)}, f32[5,1024]{1,0:T(8,128)S(1)}, u32[]{:S(2)}, u32[]{:S(2)}) collective-permute-start(f32[5,1024]{1,0:T(8,128)S(1)} %multiply_reduce_fusion), channel_id=1, source_target_pairs={{0,1},{1,0},{2,3},{3,2},{4,5},{5,4},{6,7},{7,6},{8,9},{9,8},{10,11... | collective-permute-start | bytes 61448 | tf_op jit(solution)/shard_map/ppermute | solution.py:57
  17.3 23.5 %all-to-all-start = ((s32[1,8,512]{2,0,1:T(1,128)}), s32[1,8,512]{2,0,1:T(1,128)S(1)}, u32[]{:S(2)}, u32[]{:S(2)}) async-start(s32[1,8,512]{2,0,1:T(1,128)} %bitcast.12), calls=%async_computation | async-start | bytes 32768 | tf_op jit(solution)/shard_map/all_to_all | solution.py:81
  21.1 12.3 %collective-permute-start.2 = (f32[5,2,1,128]{3,0,2,1:T(8,128)S(1)}, f32[5,2,1,128]{3,0,2,1:T(8,128)S(1)}, u32[]{:S(2)}, u32[]{:S(2)}) collective-permute-start(f32[5,2,1,128]{3,0,2,1:T(8,128)S(1)} %get-tuple-element.13), channel_id=1, source_target_pairs={{1,0},{2,1},{3,2},{5,4},{6,5},{7,6},{9,8},{10,9},{11,10},{13,12},{... | collective-permute-start | bytes 15368 | tf_op jit(solution)/shard_map/ppermute | solution.py:23
  22.4 11.0 %collective-permute-start.3 = (f32[5,2,1,128]{3,0,2,1:T(8,128)S(1)}, f32[5,2,1,128]{3,0,2,1:T(8,128)S(1)}, u32[]{:S(2)}, u32[]{:S(2)}) collective-permute-start(f32[5,2,1,128]{3,0,2,1:T(8,128)S(1)} %get-tuple-element.12), channel_id=1, source_target_pairs={{0,1},{1,2},{2,3},{4,5},{5,6},{6,7},{8,9},{9,10},{10,11},{12,13},{... | collective-permute-start | bytes 15368 | tf_op jit(solution)/shard_map/ppermute | solution.py:21
  27.6 47.8 %collective-permute-start = (f32[5,1,16,128]{3,0,2,1:T(8,128)}, f32[5,1,16,128]{3,0,2,1:T(8,128)S(1)}, u32[]{:S(2)}, u32[]{:S(2)}) collective-permute-start(f32[5,1,16,128]{3,0,2,1:T(8,128)} %get-tuple-element.11), channel_id=1, source_target_pairs={{4,0},{8,4},{12,8},{16,12},{20,16},{24,20},{28,24},{0,28},{5,1},{9... | collective-permute-start | bytes 122888 | tf_op jit(solution)/shard_map/ppermute | solution.py:23
  29.6 45.7 %collective-permute-start.1 = (f32[5,1,16,128]{3,0,2,1:T(8,128)S(1)}, f32[5,1,16,128]{3,0,2,1:T(8,128)S(1)}, u32[]{:S(2)}, u32[]{:S(2)}) collective-permute-start(f32[5,1,16,128]{3,0,2,1:T(8,128)S(1)} %get-tuple-element.10), channel_id=1, source_target_pairs={{0,4},{4,8},{8,12},{12,16},{16,20},{20,24},{24,28},{28,0},{1,5},{5... | collective-permute-start | bytes 122888 | tf_op jit(solution)/shard_map/ppermute | solution.py:21
  30.7 4.9 %collective-permute-start.5 = (f32[5,1024]{1,0:T(8,128)S(1)}, f32[5,1024]{1,0:T(8,128)S(1)}, u32[]{:S(2)}, u32[]{:S(2)}) collective-permute-start(f32[5,1024]{1,0:T(8,128)S(1)} %add.185), channel_id=1, source_target_pairs={{0,2},{1,3},{2,0},{3,1},{4,6},{5,7},{6,4},{7,5},{8,10},{9,11},{10,... | collective-permute-start | bytes 61448 | tf_op jit(solution)/shard_map/ppermute | solution.py:57
  35.6 5.1 %copy-start.2 = (f32[5,1024]{1,0:T(8,128)}, f32[5,1024]{1,0:T(8,128)S(1)}, u32[]{:S(2)}) copy-start(f32[5,1024]{1,0:T(8,128)S(1)} %add.186) | copy-start | bytes 61444
  40.7 8.8 %all-to-all-start.1 = ((f32[5,8,512]{2,0,1:T(8,128)}), f32[5,8,512]{2,0,1:T(8,128)S(1)}, u32[]{:S(2)}, u32[]{:S(2)}) async-start(f32[5,8,512]{2,0,1:T(8,128)} %copy.94), calls=%async_computation.1 | async-start | bytes 262144 | tf_op jit(solution)/shard_map/all_to_all | solution.py:80
  51.5 23.8 %copy-start.3 = (f32[5,2,16,128]{3,0,2,1:T(8,128)S(1)}, f32[5,2,16,128]{3,0,2,1:T(8,128)}, u32[]{:S(2)}) copy-start(f32[5,2,16,128]{3,0,2,1:T(8,128)} %fusion.10) | copy-start | bytes 245764
  51.5 23.8 %copy-start.4 = (f32[5,2,16,128]{3,0,2,1:T(8,128)S(1)}, f32[5,2,16,128]{3,0,2,1:T(8,128)}, u32[]{:S(2)}) copy-start(f32[5,2,16,128]{3,0,2,1:T(8,128)} %fusion.9) | copy-start | bytes 245764
  51.5 23.8 %copy-start.7 = (f32[2,16,128]{2,1,0:T(8,128)S(1)}, f32[2,16,128]{2,1,0:T(8,128)}, u32[]{:S(2)}) copy-start(f32[2,16,128]{2,1,0:T(8,128)} %param.16) | copy-start | bytes 49156
